TPU v7x, 32 devices: a whole 2x2x4 slice. The times are simulated.
32 devices in a mesh: dp: 4 (over y, x), seq: 2 (over core), tensor: 4 (over z).
Axes of the slice: x: 2, y: 2, z: 4, core: 2. Of those that a mesh axis runs over, the one named last changes fastest.
Arguments:
- block_input: float32 [4, 16, 256, 1024], P('dp', 'seq', 'tensor'), may hold values from -6 to 6
- w_qkv: bfloat16 [1024, 3, 1024], P(None, None, 'tensor'), may hold values from -0.1875 to 0.1875
- qv_bias: bfloat16 [2, 1024], P(None, 'tensor'), may hold values from -3 to 3
- w_out: bfloat16 [1024, 1024], P('tensor'), may hold values from -3 to 3
- b_out: bfloat16 [1024], replicated, may hold values from -3 to 3
- w_up: bfloat16 [1024, 4096], P(None, 'tensor'), may hold values from -0.1875 to 0.1875
- b_up: bfloat16 [4096], P('tensor'), may hold values from -3 to 3
- w_down: bfloat16 [4096, 1024], P('tensor'), may hold values from -0.09375 to 0.09375
- b_down: bfloat16 [1024], replicated, may hold values from -3 to 3
- w_mod: bfloat16 [1024, 6144], replicated, may hold values from -0.375 to 0.375
- b_mod: bfloat16 [6144], replicated, may hold values from -3 to 3
- context_frames: int32 [4], P('dp'), may hold values from 1 to 15
- noise_levels: int32 [4, 16], P('dp', 'seq'), may hold values from 0 to 999
- cotangent: float32 [4, 16, 256, 1024], P('dp', 'seq', 'tensor'), may hold values from -6 to 6
Outputs:
- output: float32 [4, 16, 256, 1024], P('dp', 'seq', 'tensor')
- grad_input: float32 [4, 16, 256, 1024], P('dp', 'seq', 'tensor')
- grad_w_qkv: float32 [1024, 3, 1024], P(None, None, 'tensor')
- grad_qv_bias: float32 [2, 1024], P(None, 'tensor')
- grad_w_out: float32 [1024, 1024], P('tensor')
- grad_b_out: float32 [1024], P('tensor')
- grad_w_up: float32 [1024, 4096], P(None, 'tensor')
- grad_b_up: float32 [4096], P('tensor')
- grad_w_down: float32 [4096, 1024], P('tensor')
- grad_b_down: float32 [1024], P('tensor')
- grad_w_mod: float32 [1024, 6144], P(None, 'tensor')
- grad_b_mod: float32 [6144], P('tensor')
Inputs may be any that keep to these rules, and one draw needn't show every extreme that they name: `noise_levels`: noise level index of each frame.
All inputs are finite; a program needn't handle non-finite values.
Results may differ from a plain program's by a relative error of at most 0.02.
Values may be sent and summed in bfloat16 or wider, within the bound.
No kernel may reach another device: no remote copies, remote signals or barrier semaphores. Data moves between devices by JAX's collectives and lax.ppermute only.
A program may use at most 256 MiB of HBM per device.

v0:
```python
import math
import jax
import jax.numpy as jnp
from jax import lax
from jax.sharding import PartitionSpec as P

HD = 64


def level_features(levels, context, frame_ids, breadth):
    level_used = jnp.where(frame_ids[None, :] < context[:, None], 0, levels).astype(jnp.float32)
    halfway = breadth // 2
    frequency = jnp.exp(-math.log(10000.0) * jnp.arange(halfway, dtype=jnp.float32) / halfway)
    angles = level_used[..., None] * frequency
    return jax.nn.silu(jnp.concatenate([jnp.cos(angles), jnp.sin(angles)], axis=-1))


def normalize(stream):
    centre = stream - jnp.mean(stream, axis=-1, keepdims=True)
    inverse = lax.rsqrt(jnp.mean(centre * centre, axis=-1, keepdims=True) + 1e-06)
    return (centre * inverse, inverse)


def norm_back(grad_normed, normed, inverse):
    first_mean = jnp.mean(grad_normed, axis=-1, keepdims=True)
    second_mean = jnp.mean(grad_normed * normed, axis=-1, keepdims=True)
    return inverse * (grad_normed - first_mean - normed * second_mean)


def gelu_back(pre_act, grad_act):
    _, pullback = jax.vjp(lambda argument: jax.nn.gelu(argument, approximate=True), pre_act)
    return pullback(grad_act)[0]


def body(
    block_input,
    w_qkv,
    qv_bias,
    w_out,
    b_out,
    w_up,
    b_up,
    w_down,
    b_down,
    w_mod,
    b_mod,
    context_frames,
    noise_levels,
    cotangent,
):
    clip_count, half_frames, patch_local, breadth = block_input.shape
    patches_all = patch_local * lax.axis_size("tensor")
    head_cols = w_qkv.shape[2]
    heads_local = head_cols // HD
    softmax_scale = HD ** (-0.5)
    frame_first = lax.axis_index("seq") * half_frames
    frame_ids = frame_first + jnp.arange(half_frames, dtype=jnp.int32)
    condition = level_features(noise_levels, context_frames, frame_ids, breadth).astype(
        jnp.bfloat16
    )
    modulation = jnp.einsum(
        "cfd,de->cfe", condition, w_mod, preferred_element_type=jnp.float32
    ) + b_mod.astype(jnp.float32)
    shift_one, scale_one, gate_one, shift_two, scale_two, gate_two = jnp.split(
        modulation[:, :, None, :], 6, axis=-1
    )
    normed_one, inverse_one = normalize(block_input)
    attn_in = (normed_one * (1.0 + scale_one) + shift_one).astype(jnp.bfloat16)
    attn_all = lax.all_gather(attn_in, "tensor", axis=2, tiled=True)
    projected = jnp.einsum("cfpd,dke->cfpke", attn_all, w_qkv, preferred_element_type=jnp.float32)
    bias_float = qv_bias.astype(jnp.float32)
    queries = (projected[..., 0, :] + bias_float[0]).astype(jnp.bfloat16)
    key_local = projected[..., 1, :].astype(jnp.bfloat16)
    value_local = (projected[..., 2, :] + bias_float[1]).astype(jnp.bfloat16)
    key_clip, value_clip = (
        lax.all_gather(key_local, "seq", axis=1, tiled=True),
        lax.all_gather(value_local, "seq", axis=1, tiled=True),
    )
    query_rows = half_frames * patches_all
    block_rows = min(512, query_rows)
    block_count = query_rows // block_rows
    key_rows = key_clip.shape[1] * patches_all
    key_frame = jnp.arange(key_rows, dtype=jnp.int32) // patches_all
    query_frames = (frame_first + jnp.arange(query_rows, dtype=jnp.int32) // patches_all).reshape(
        block_count, block_rows
    )
    query_heads = queries.reshape(clip_count, block_count, block_rows, heads_local, HD)
    key_heads = key_clip.reshape(clip_count, key_rows, heads_local, HD)
    value_heads = value_clip.reshape(clip_count, key_rows, heads_local, HD)

    def masked_scores(query_block, keys, frames_block, context_limit):
        scores = (
            jnp.einsum("bhd,khd->hbk", query_block, keys, preferred_element_type=jnp.float32)
            * softmax_scale
        )
        allowed = (key_frame[None, :] <= frames_block[:, None]) | (
            key_frame[None, :] < context_limit
        )
        return jnp.where(allowed[None], scores, -1e30)

    def forward_clip(members):
        clip_queries, keys, values, context_limit = members

        def forward_block(slices):
            query_block, frames_block = slices
            scores = masked_scores(query_block, keys, frames_block, context_limit)
            row_max = jnp.max(scores, axis=-1, keepdims=True)
            exponent = jnp.exp(scores - row_max)
            denominator = jnp.sum(exponent, axis=-1, keepdims=True)
            probability = (exponent / denominator).astype(jnp.bfloat16)
            result = jnp.einsum(
                "hbk,khd->bhd", probability, values, preferred_element_type=jnp.float32
            )
            return (result.astype(jnp.bfloat16), (row_max + jnp.log(denominator))[..., 0])

        return lax.map(forward_block, (clip_queries, query_frames))

    attended, log_total = lax.map(
        forward_clip, (query_heads, key_heads, value_heads, context_frames)
    )
    attended_rows = attended.reshape(clip_count, half_frames, patches_all, head_cols)
    portion = attended_rows
    branch_rows = lax.psum_scatter(
        jnp.einsum("cfpe,ed->pcfd", portion, w_out, preferred_element_type=jnp.float32).astype(
            jnp.bfloat16
        ),
        "tensor",
        scatter_dimension=0,
        tiled=True,
    ).astype(jnp.float32)
    branch_one = jnp.transpose(branch_rows, (1, 2, 0, 3)) + b_out.astype(jnp.float32)
    hidden_one = block_input + gate_one * branch_one
    normed_two, inverse_two = normalize(hidden_one)
    mlp_in = (normed_two * (1.0 + scale_two) + shift_two).astype(jnp.bfloat16)
    mlp_all = lax.all_gather(mlp_in, "tensor", axis=2, tiled=True)
    pre_act = jnp.einsum(
        "cfpd,de->cfpe", mlp_all, w_up, preferred_element_type=jnp.float32
    ) + b_up.astype(jnp.float32)
    activated = jax.nn.gelu(pre_act, approximate=True).astype(jnp.bfloat16)
    portion = activated
    mlp_rows = lax.psum_scatter(
        jnp.einsum("cfpe,ed->pcfd", portion, w_down, preferred_element_type=jnp.float32).astype(
            jnp.bfloat16
        ),
        "tensor",
        scatter_dimension=0,
        tiled=True,
    ).astype(jnp.float32)
    mlp_out = jnp.transpose(mlp_rows, (1, 2, 0, 3)) + b_down.astype(jnp.float32)
    output = hidden_one + gate_two * mlp_out
    grad_mlp = gate_two * cotangent
    grad_gate_two = jnp.sum(cotangent * mlp_out, axis=2)
    grad_b_down = jnp.sum(grad_mlp, axis=(0, 1, 2))
    grad_mlp_low = grad_mlp.astype(jnp.bfloat16)
    grad_mlp_all = lax.all_gather(grad_mlp_low, "tensor", axis=2, tiled=True)
    grad_act = jnp.einsum("cfpd,ed->cfpe", grad_mlp_all, w_down, preferred_element_type=jnp.float32)
    grad_w_down = jnp.einsum(
        "cfpe,cfpd->ed", activated, grad_mlp_all, preferred_element_type=jnp.float32
    )
    grad_pre = gelu_back(pre_act, grad_act).astype(jnp.bfloat16)
    grad_b_up = jnp.sum(grad_pre.astype(jnp.float32), axis=(0, 1, 2))
    grad_w_up = jnp.einsum("cfpd,cfpe->de", mlp_all, grad_pre, preferred_element_type=jnp.float32)
    portion = grad_pre
    grad_mlp_rows = lax.psum_scatter(
        jnp.einsum("cfpe,de->pcfd", portion, w_up, preferred_element_type=jnp.float32).astype(
            jnp.bfloat16
        ),
        "tensor",
        scatter_dimension=0,
        tiled=True,
    ).astype(jnp.float32)
    grad_mlp_in = jnp.transpose(grad_mlp_rows, (1, 2, 0, 3))
    grad_shift_two = jnp.sum(grad_mlp_in, axis=2)
    grad_scale_two = jnp.sum(grad_mlp_in * normed_two, axis=2)
    grad_hidden = cotangent + norm_back(grad_mlp_in * (1.0 + scale_two), normed_two, inverse_two)
    grad_branch = gate_one * grad_hidden
    grad_gate_one = jnp.sum(grad_hidden * branch_one, axis=2)
    grad_b_out = jnp.sum(grad_branch, axis=(0, 1, 2))
    grad_branch_all = lax.all_gather(grad_branch.astype(jnp.bfloat16), "tensor", axis=2, tiled=True)
    grad_attended = jnp.einsum(
        "cfpd,ed->cfpe", grad_branch_all, w_out, preferred_element_type=jnp.float32
    ).astype(jnp.bfloat16)
    grad_w_out = jnp.einsum(
        "cfpe,cfpd->ed", attended_rows, grad_branch_all, preferred_element_type=jnp.float32
    )
    grad_heads = grad_attended.reshape(clip_count, block_count, block_rows, heads_local, HD)

    def backward_clip(members):
        clip_queries, keys, values, context_limit, clip_grads, clip_totals = members

        def backward_block(running, slices):
            key_acc, value_acc = running
            query_block, frames_block, grad_block, total_block = slices
            scores = masked_scores(query_block, keys, frames_block, context_limit)
            probability = jnp.exp(scores - total_block[..., None])
            grad_prob = jnp.einsum(
                "bhd,khd->hbk", grad_block, values, preferred_element_type=jnp.float32
            )
            inner_sum = jnp.sum(probability * grad_prob, axis=-1, keepdims=True)
            grad_scores = (probability * (grad_prob - inner_sum)).astype(jnp.bfloat16)
            grad_query = (
                jnp.einsum("hbk,khd->bhd", grad_scores, keys, preferred_element_type=jnp.float32)
                * softmax_scale
            )
            key_acc = (
                key_acc
                + jnp.einsum(
                    "hbk,bhd->khd", grad_scores, query_block, preferred_element_type=jnp.float32
                )
                * softmax_scale
            )
            value_acc = value_acc + jnp.einsum(
                "hbk,bhd->khd",
                probability.astype(jnp.bfloat16),
                grad_block,
                preferred_element_type=jnp.float32,
            )
            return ((key_acc, value_acc), grad_query.astype(jnp.bfloat16))

        empty_acc = jnp.zeros((key_rows, heads_local, HD), jnp.float32)
        (grad_keys, grad_values), grad_queries = lax.scan(
            backward_block,
            (empty_acc, empty_acc),
            (clip_queries, query_frames, clip_grads, clip_totals),
        )
        return (grad_queries, grad_keys, grad_values)

    grad_queries, grad_keys, grad_values = lax.map(
        backward_clip, (query_heads, key_heads, value_heads, context_frames, grad_heads, log_total)
    )
    key_shape = (clip_count, key_clip.shape[1], patches_all, head_cols)
    grad_key_own, grad_value_own = (
        lax.psum_scatter(
            grad_keys.reshape(key_shape).astype(jnp.bfloat16),
            "seq",
            scatter_dimension=1,
            tiled=True,
        ).astype(jnp.float32),
        lax.psum_scatter(
            grad_values.reshape(key_shape).astype(jnp.bfloat16),
            "seq",
            scatter_dimension=1,
            tiled=True,
        ).astype(jnp.float32),
    )
    grad_qkv = jnp.stack(
        [
            grad_queries.reshape(clip_count, half_frames, patches_all, head_cols),
            grad_key_own.astype(jnp.bfloat16),
            grad_value_own.astype(jnp.bfloat16),
        ],
        axis=3,
    )
    grad_w_qkv = jnp.einsum(
        "cfpd,cfpke->dke", attn_all, grad_qkv, preferred_element_type=jnp.float32
    )
    grad_qv_bias = jnp.sum(grad_qkv[:, :, :, 0::2, :].astype(jnp.float32), axis=(0, 1, 2))
    portion = grad_qkv
    grad_attn_rows = lax.psum_scatter(
        jnp.einsum("cfpke,dke->pcfd", portion, w_qkv, preferred_element_type=jnp.float32).astype(
            jnp.bfloat16
        ),
        "tensor",
        scatter_dimension=0,
        tiled=True,
    ).astype(jnp.float32)
    grad_attn_in = jnp.transpose(grad_attn_rows, (1, 2, 0, 3))
    grad_shift_one = jnp.sum(grad_attn_in, axis=2)
    grad_scale_one = jnp.sum(grad_attn_in * normed_one, axis=2)
    grad_input = grad_hidden + norm_back(grad_attn_in * (1.0 + scale_one), normed_one, inverse_one)
    grad_modulation = jnp.concatenate(
        [
            grad_shift_one,
            grad_scale_one,
            grad_gate_one,
            grad_shift_two,
            grad_scale_two,
            grad_gate_two,
        ],
        axis=-1,
    )
    grad_modulation = grad_modulation.reshape(clip_count * half_frames, 6 * breadth)
    modulation_cols, out_bias_part, down_bias_part = (
        lax.psum_scatter(
            grad_modulation.astype(jnp.bfloat16), "tensor", scatter_dimension=1, tiled=True
        ).astype(jnp.float32),
        lax.psum_scatter(
            grad_b_out.astype(jnp.bfloat16), "tensor", scatter_dimension=0, tiled=True
        ).astype(jnp.float32),
        lax.psum_scatter(
            grad_b_down.astype(jnp.bfloat16), "tensor", scatter_dimension=0, tiled=True
        ).astype(jnp.float32),
    )
    condition_rows = condition.reshape(clip_count * half_frames, breadth).astype(jnp.float32)
    grad_w_mod = jnp.dot(condition_rows.T, modulation_cols, precision=lax.Precision.HIGHEST)
    grad_b_mod = jnp.sum(modulation_cols, axis=0)
    (
        total_w_qkv,
        total_qv_bias,
        total_w_out,
        total_b_out,
        total_w_up,
        total_b_up,
        total_w_down,
        total_b_down,
        total_w_mod,
        total_b_mod,
    ) = (
        lax.psum(grad_w_qkv.astype(jnp.bfloat16), ("dp", "seq")).astype(jnp.float32),
        lax.psum(grad_qv_bias.astype(jnp.bfloat16), ("dp", "seq")).astype(jnp.float32),
        lax.psum(grad_w_out.astype(jnp.bfloat16), ("dp", "seq")).astype(jnp.float32),
        lax.psum(out_bias_part.astype(jnp.bfloat16), ("dp", "seq")).astype(jnp.float32),
        lax.psum(grad_w_up.astype(jnp.bfloat16), ("dp", "seq")).astype(jnp.float32),
        lax.psum(grad_b_up.astype(jnp.bfloat16), ("dp", "seq")).astype(jnp.float32),
        lax.psum(grad_w_down.astype(jnp.bfloat16), ("dp", "seq")).astype(jnp.float32),
        lax.psum(down_bias_part.astype(jnp.bfloat16), ("dp", "seq")).astype(jnp.float32),
        lax.psum(grad_w_mod.astype(jnp.bfloat16), ("dp", "seq")).astype(jnp.float32),
        lax.psum(grad_b_mod.astype(jnp.bfloat16), ("dp", "seq")).astype(jnp.float32),
    )
    return (
        output,
        grad_input,
        total_w_qkv,
        total_qv_bias,
        total_w_out,
        total_b_out,
        total_w_up,
        total_b_up,
        total_w_down,
        total_b_down,
        total_w_mod,
        total_b_mod,
    )


def solution(mesh):
    placed = (
        P("dp", "seq", "tensor", None),
        P(None, None, "tensor"),
        P(None, "tensor"),
        P("tensor", None),
        P(),
        P(None, "tensor"),
        P("tensor"),
        P("tensor", None),
        P(),
        P(),
        P(),
        P("dp"),
        P("dp", "seq"),
        P("dp", "seq", "tensor", None),
    )
    return jax.shard_map(
        body,
        mesh=mesh,
        in_specs=placed,
        out_specs=(
            P("dp", "seq", "tensor", None),
            P("dp", "seq", "tensor", None),
            P(None, None, "tensor"),
            P(None, "tensor"),
            P("tensor", None),
            P("tensor"),
            P(None, "tensor"),
            P("tensor"),
            P("tensor", None),
            P("tensor"),
            P(None, "tensor"),
            P("tensor"),
        ),
        check_vma=False,
    )
```

profile of v0, /device:TPU:0, one launch (start us, length us, event | category | flops | bytes accessed | tf_op | source)
XLA Modules:
  0.0 1632.9 jit_solution(15091767421687436867)
XLA Ops:
  21.3 83.5 %all-gather.8.cloned.1.call-done = bf16[1,8,256,1024]{3,2,1,0:T(8,128)(2,1)} async-done(((bf16[1,8,64,1024]{3,2,1,0:T(8,128)(2,1)}), bf16[1,8,256,1024]{3,2,1,0:T(8,128)(2,1)}) %all-gather.8.cloned.1.call-update) | async-done | bytes 4194320 | tf_op jit(solution)/shard_map/all_gather | solution.py:69
  147.6 198.6 %while.50 = (s32[]{:T(128)}, bf16[4,512,4,64]{1,3,2,0:T(8,128)(2,1)S(1)}, f32[4,4,512]{2,1,0:T(4,128)S(1)}, s32[4,512]{1,0:T(4,128)S(1)}, s32[]{:T(128)}, /*inde...) while((s32[]{:T(128)}, ...), condition=%wide.region_5.6_spmd.clone.clone, body=%wide.region_2.5_spmd.clone.clone.sunk | while | flops 2252539904 | bytes 122271888 | solution.py:116
  150.0 16.0 fusion.176
  166.1 15.0 fusion.177
  181.1 16.3 fusion.178
  199.6 16.0 fusion.176
  215.7 15.0 fusion.177
  230.7 16.3 fusion.178
  249.2 16.0 fusion.176
  265.3 15.0 fusion.177
  280.3 16.3 fusion.178
  298.8 16.0 fusion.176
  314.9 15.0 fusion.177
  329.9 16.3 fusion.178
  354.7 76.7 %reduce-scatter.8.cloned.1.call-done = bf16[64,1,8,1024]{3,0,2,1:T(8,128)(2,1)} async-done(((bf16[256,1,8,1024]{3,0,2,1:T(8,128)(2,1)}), bf16[64,1,8,1024]{3,0,2,1:T(8,128)(2,1)}) %reduce-scatter.8.cloned.1.call-update) | async-done | bytes 1048592 | tf_op jit(solution)/shard_map/reduce_scatter | solution.py:123
  436.6 81.3 %all-gather.12.cloned.1.call-done = bf16[1,8,256,1024]{3,2,1,0:T(8,128)(2,1)} async-done(((bf16[1,8,64,1024]{3,2,1,0:T(8,128)(2,1)}), bf16[1,8,256,1024]{3,2,1,0:T(8,128)(2,1)}) %all-gather.12.cloned.1.call-update) | async-done | bytes 4194320 | tf_op jit(solution)/shard_map/all_gather | solution.py:135
  535.7 74.8 %reduce-scatter.10.cloned.1.call-done = bf16[64,1,8,1024]{3,0,2,1:T(8,128)(2,1)} async-done(((bf16[256,1,8,1024]{3,0,2,1:T(8,128)(2,1)}), bf16[64,1,8,1024]{3,0,2,1:T(8,128)(2,1)}) %reduce-scatter.10.cloned.1.call-update) | async-done | bytes 1048592 | tf_op jit(solution)/shard_map/reduce_scatter | solution.py:141
  614.5 81.4 %all-gather.14.cloned.1.call-done = bf16[1,8,256,1024]{3,2,1,0:T(8,128)(2,1)} async-done(((bf16[1,8,64,1024]{3,2,1,0:T(8,128)(2,1)}), bf16[1,8,256,1024]{3,2,1,0:T(8,128)(2,1)}) %all-gather.14.cloned.1.call-update) | async-done | bytes 4194320 | tf_op jit(solution)/shard_map/all_gather | solution.py:155
  695.9 13.3 fusion.144
  717.5 75.4 %reduce-scatter.12.cloned.1.call-done = bf16[64,1,8,1024]{3,0,2,1:T(8,128)(2,1)} async-done(((bf16[256,1,8,1024]{3,0,2,1:T(8,128)(2,1)}), bf16[64,1,8,1024]{3,0,2,1:T(8,128)(2,1)}) %reduce-scatter.12.cloned.1.call-update) | async-done | bytes 1048592 | tf_op jit(solution)/shard_map/reduce_scatter | solution.py:164
  803.0 81.3 %all-gather.16.cloned.1.call-done = bf16[1,8,256,1024]{3,2,1,0:T(8,128)(2,1)} async-done(((bf16[1,8,64,1024]{3,2,1,0:T(8,128)(2,1)}), bf16[1,8,256,1024]{3,2,1,0:T(8,128)(2,1)}) %all-gather.16.cloned.1.call-update) | async-done | bytes 4194320 | tf_op jit(solution)/shard_map/all_gather | solution.py:179
  892.2 435.7 %while.51 = (s32[]{:T(128)}, f32[4096,4,64]{0,2,1:T(8,128)}, f32[4096,4,64]{0,2,1:T(8,128)}, bf16[4,512,4,64]{1,3,2,0:T(8,128)(2,1)}, bf16[4,512,4,64]{1,3,2,0:T...) while((s32[]{:T(128)}, f32[4096,4,64]{0,2,1:T(8,128)}, ...), condition=%wide.region_15.16_spmd.clone.clone, body=%wide.region_13.15_spmd.clone.clone.sunk | while | flops 5504305152 | bytes 351639744 | solution.py:221
  894.6 17.3 %fusion.188 = f32[4,512,4096]{2,1,0:T(8,128)} fusion(bf16[4096,4,64]{0,2,1:T(8,128)(2,1)} %get-tuple-element.645, bf16[4,512,4,64]{1,3,2,0:T(8,128)(2,1)} %get-tuple-element.642, s32[]{:T(128)S(6)} %copy.131), kind=kOutput, calls=%fused_computation.48.clone.1 | convolution fusion | flops 1073741824 | bytes 35913732 | tf_op jit(solution)/shard_map/while/body/eval_jaxpr/while/body/eval_jaxpr/bhd,khd->hbk/dot_general | solution.py:93
  911.9 16.5 %fusion.190 = f32[4096,4,64]{0,2,1:T(8,128)} fusion(f32[4,512,4096]{2,1,0:T(8,128)} %fusion.188, f32[4,512]{1,0:T(4,128)S(1)} %dynamic-slice_bitcast_fusion.2, pred[512,4096]{1,0:T(8,128)(4,1)S(1)} %compare_or_fusion.5, f32[4096,4,64]{0,2,1:T(8,128)} %get-tuple-element.627, pred[]{:T(512)S(6)} %compare.9, ...), kind=kOutput, calls=%fused_computation.39.clone.1 | convolution fusion | flops 1109393408 | bytes 44310532 | tf_op jit(solution)/shard_map/while/body/eval_jaxpr/while/body/eval_jaxpr/hbk,bhd->khd/dot_general | solution.py:212
  928.4 25.9 %multiply_reduce_fusion.6 = (f32[4,512]{1,0:T(4,128)S(1)}, f32[4,512,4096]{2,1,0:T(8,128)}) fusion(f32[4,512,4096]{2,1,0:T(8,128)} %fusion.188, f32[4,512]{1,0:T(4,128)S(1)} %dynamic-slice_bitcast_fusion.2, pred[512,4096]{1,0:T(8,128)(4,1)S(1)} %compare_or_fusion.5, bf16[4096,4,64]{0,2,1:T(8,128)(2,1)} %get-tuple-element.648, ...), kind=kOutput, calls=%fused_computation.29.clone.1 | convolution fusion | flops 1115682816 | bytes 71581696 | tf_op jit(solution)/shard_map/while/body/eval_jaxpr/while/body/eval_jaxpr/bhd,khd->hbk/dot_general | solution.py:196
  954.3 27.6 %multiply_convert_fusion.10 = bf16[4,512,4096]{2,1,0:T(8,128)(2,1)} fusion(f32[4,512,4096]{2,1,0:T(8,128)} %get-tuple-element.583, f32[4,512,4096]{2,1,0:T(8,128)} %fusion.188, f32[4,512]{1,0:T(4,128)S(1)} %get-tuple-element.584, f32[4,512]{1,0:T(4,128)S(1)} %dynamic-slice_bitcast_fusion.2, pred[512,4096]{1,0:T(8,128)(4,1)S(1)} %compare_or_fusion.5), kind=kLoop, calls=%fused_computation.28.clone.1 | loop fusion | flops 50331648 | bytes 85999616 | tf_op jit(solution)/shard_map/while/body/eval_jaxpr/while/body/eval_jaxpr/convert_element_type | solution.py:200
  981.9 10.1 fusion.191
  1001.5 17.3 %fusion.188 = f32[4,512,4096]{2,1,0:T(8,128)} fusion(bf16[4096,4,64]{0,2,1:T(8,128)(2,1)} %get-tuple-element.645, bf16[4,512,4,64]{1,3,2,0:T(8,128)(2,1)} %get-tuple-element.642, s32[]{:T(128)S(6)} %copy.131), kind=kOutput, calls=%fused_computation.48.clone.1 | convolution fusion | flops 1073741824 | bytes 35913732 | tf_op jit(solution)/shard_map/while/body/eval_jaxpr/while/body/eval_jaxpr/bhd,khd->hbk/dot_general | solution.py:93
  1018.8 17.7 %fusion.190 = f32[4096,4,64]{0,2,1:T(8,128)} fusion(f32[4,512,4096]{2,1,0:T(8,128)} %fusion.188, f32[4,512]{1,0:T(4,128)S(1)} %dynamic-slice_bitcast_fusion.2, pred[512,4096]{1,0:T(8,128)(4,1)S(1)} %compare_or_fusion.5, f32[4096,4,64]{0,2,1:T(8,128)} %get-tuple-element.627, pred[]{:T(512)S(6)} %compare.9, ...), kind=kOutput, calls=%fused_computation.39.clone.1 | convolution fusion | flops 1109393408 | bytes 44310532 | tf_op jit(solution)/shard_map/while/body/eval_jaxpr/while/body/eval_jaxpr/hbk,bhd->khd/dot_general | solution.py:212
  1036.5 25.9 %multiply_reduce_fusion.6 = (f32[4,512]{1,0:T(4,128)S(1)}, f32[4,512,4096]{2,1,0:T(8,128)}) fusion(f32[4,512,4096]{2,1,0:T(8,128)} %fusion.188, f32[4,512]{1,0:T(4,128)S(1)} %dynamic-slice_bitcast_fusion.2, pred[512,4096]{1,0:T(8,128)(4,1)S(1)} %compare_or_fusion.5, bf16[4096,4,64]{0,2,1:T(8,128)(2,1)} %get-tuple-element.648, ...), kind=kOutput, calls=%fused_computation.29.clone.1 | convolution fusion | flops 1115682816 | bytes 71581696 | tf_op jit(solution)/shard_map/while/body/eval_jaxpr/while/body/eval_jaxpr/bhd,khd->hbk/dot_general | solution.py:196
  1062.4 27.6 %multiply_convert_fusion.10 = bf16[4,512,4096]{2,1,0:T(8,128)(2,1)} fusion(f32[4,512,4096]{2,1,0:T(8,128)} %get-tuple-element.583, f32[4,512,4096]{2,1,0:T(8,128)} %fusion.188, f32[4,512]{1,0:T(4,128)S(1)} %get-tuple-element.584, f32[4,512]{1,0:T(4,128)S(1)} %dynamic-slice_bitcast_fusion.2, pred[512,4096]{1,0:T(8,128)(4,1)S(1)} %compare_or_fusion.5), kind=kLoop, calls=%fused_computation.28.clone.1 | loop fusion | flops 50331648 | bytes 85999616 | tf_op jit(solution)/shard_map/while/body/eval_jaxpr/while/body/eval_jaxpr/convert_element_type | solution.py:200
  1090.0 10.1 fusion.191
  1110.9 17.3 %fusion.188 = f32[4,512,4096]{2,1,0:T(8,128)} fusion(bf16[4096,4,64]{0,2,1:T(8,128)(2,1)} %get-tuple-element.645, bf16[4,512,4,64]{1,3,2,0:T(8,128)(2,1)} %get-tuple-element.642, s32[]{:T(128)S(6)} %copy.131), kind=kOutput, calls=%fused_computation.48.clone.1 | convolution fusion | flops 1073741824 | bytes 35913732 | tf_op jit(solution)/shard_map/while/body/eval_jaxpr/while/body/eval_jaxpr/bhd,khd->hbk/dot_general | solution.py:93
  1128.2 17.7 %fusion.190 = f32[4096,4,64]{0,2,1:T(8,128)} fusion(f32[4,512,4096]{2,1,0:T(8,128)} %fusion.188, f32[4,512]{1,0:T(4,128)S(1)} %dynamic-slice_bitcast_fusion.2, pred[512,4096]{1,0:T(8,128)(4,1)S(1)} %compare_or_fusion.5, f32[4096,4,64]{0,2,1:T(8,128)} %get-tuple-element.627, pred[]{:T(512)S(6)} %compare.9, ...), kind=kOutput, calls=%fused_computation.39.clone.1 | convolution fusion | flops 1109393408 | bytes 44310532 | tf_op jit(solution)/shard_map/while/body/eval_jaxpr/while/body/eval_jaxpr/hbk,bhd->khd/dot_general | solution.py:212
  1145.9 25.9 %multiply_reduce_fusion.6 = (f32[4,512]{1,0:T(4,128)S(1)}, f32[4,512,4096]{2,1,0:T(8,128)}) fusion(f32[4,512,4096]{2,1,0:T(8,128)} %fusion.188, f32[4,512]{1,0:T(4,128)S(1)} %dynamic-slice_bitcast_fusion.2, pred[512,4096]{1,0:T(8,128)(4,1)S(1)} %compare_or_fusion.5, bf16[4096,4,64]{0,2,1:T(8,128)(2,1)} %get-tuple-element.648, ...), kind=kOutput, calls=%fused_computation.29.clone.1 | convolution fusion | flops 1115682816 | bytes 71581696 | tf_op jit(solution)/shard_map/while/body/eval_jaxpr/while/body/eval_jaxpr/bhd,khd->hbk/dot_general | solution.py:196
  1171.8 27.6 %multiply_convert_fusion.10 = bf16[4,512,4096]{2,1,0:T(8,128)(2,1)} fusion(f32[4,512,4096]{2,1,0:T(8,128)} %get-tuple-element.583, f32[4,512,4096]{2,1,0:T(8,128)} %fusion.188, f32[4,512]{1,0:T(4,128)S(1)} %get-tuple-element.584, f32[4,512]{1,0:T(4,128)S(1)} %dynamic-slice_bitcast_fusion.2, pred[512,4096]{1,0:T(8,128)(4,1)S(1)} %compare_or_fusion.5), kind=kLoop, calls=%fused_computation.28.clone.1 | loop fusion | flops 50331648 | bytes 85999616 | tf_op jit(solution)/shard_map/while/body/eval_jaxpr/while/body/eval_jaxpr/convert_element_type | solution.py:200
  1199.4 10.1 fusion.191
  1220.3 17.3 %fusion.188 = f32[4,512,4096]{2,1,0:T(8,128)} fusion(bf16[4096,4,64]{0,2,1:T(8,128)(2,1)} %get-tuple-element.645, bf16[4,512,4,64]{1,3,2,0:T(8,128)(2,1)} %get-tuple-element.642, s32[]{:T(128)S(6)} %copy.131), kind=kOutput, calls=%fused_computation.48.clone.1 | convolution fusion | flops 1073741824 | bytes 35913732 | tf_op jit(solution)/shard_map/while/body/eval_jaxpr/while/body/eval_jaxpr/bhd,khd->hbk/dot_general | solution.py:93
  1237.6 17.7 %fusion.190 = f32[4096,4,64]{0,2,1:T(8,128)} fusion(f32[4,512,4096]{2,1,0:T(8,128)} %fusion.188, f32[4,512]{1,0:T(4,128)S(1)} %dynamic-slice_bitcast_fusion.2, pred[512,4096]{1,0:T(8,128)(4,1)S(1)} %compare_or_fusion.5, f32[4096,4,64]{0,2,1:T(8,128)} %get-tuple-element.627, pred[]{:T(512)S(6)} %compare.9, ...), kind=kOutput, calls=%fused_computation.39.clone.1 | convolution fusion | flops 1109393408 | bytes 44310532 | tf_op jit(solution)/shard_map/while/body/eval_jaxpr/while/body/eval_jaxpr/hbk,bhd->khd/dot_general | solution.py:212
  1255.3 25.9 %multiply_reduce_fusion.6 = (f32[4,512]{1,0:T(4,128)S(1)}, f32[4,512,4096]{2,1,0:T(8,128)}) fusion(f32[4,512,4096]{2,1,0:T(8,128)} %fusion.188, f32[4,512]{1,0:T(4,128)S(1)} %dynamic-slice_bitcast_fusion.2, pred[512,4096]{1,0:T(8,128)(4,1)S(1)} %compare_or_fusion.5, bf16[4096,4,64]{0,2,1:T(8,128)(2,1)} %get-tuple-element.648, ...), kind=kOutput, calls=%fused_computation.29.clone.1 | convolution fusion | flops 1115682816 | bytes 71581696 | tf_op jit(solution)/shard_map/while/body/eval_jaxpr/while/body/eval_jaxpr/bhd,khd->hbk/dot_general | solution.py:196
  1281.2 27.6 %multiply_convert_fusion.10 = bf16[4,512,4096]{2,1,0:T(8,128)(2,1)} fusion(f32[4,512,4096]{2,1,0:T(8,128)} %get-tuple-element.583, f32[4,512,4096]{2,1,0:T(8,128)} %fusion.188, f32[4,512]{1,0:T(4,128)S(1)} %get-tuple-element.584, f32[4,512]{1,0:T(4,128)S(1)} %dynamic-slice_bitcast_fusion.2, pred[512,4096]{1,0:T(8,128)(4,1)S(1)} %compare_or_fusion.5), kind=kLoop, calls=%fused_computation.28.clone.1 | loop fusion | flops 50331648 | bytes 85999616 | tf_op jit(solution)/shard_map/while/body/eval_jaxpr/while/body/eval_jaxpr/convert_element_type | solution.py:200
  1308.8 10.1 fusion.191
  1348.5 10.5 reduce-scatter.16.cloned.1.call-done
  1376.3 11.0 bitcast_convert_fusion.1
  1389.7 55.0 %reduce-scatter.18.cloned.1.call-done = bf16[64,1,8,1024]{3,0,2,1:T(8,128)(2,1)} async-done(((bf16[256,1,8,1024]{3,0,2,1:T(8,128)(2,1)}), bf16[64,1,8,1024]{3,0,2,1:T(8,128)(2,1)}) %reduce-scatter.18.cloned.1.call-update) | async-done | bytes 1048592 | tf_op jit(solution)/shard_map/reduce_scatter | solution.py:259
  1457.0 12.5 reduce-scatter.20.cloned.1.call-done
  1488.5 13.2 all-reduce.2
  1504.7 106.7 %all-reduce.7.cloned.1.call-done = (bf16[1024,3,256]{2,0,1:T(8,128)(2,1)}, bf16[256,1024]{1,0:T(8,128)(2,1)}, bf16[1024,1024]{1,0:T(8,128)(2,1)}, bf16[1024,1024]{1,0:T(8,128)(2,1)}, bf16[1024,1536]{1,0:T(8,128)(2,1)}) async-done(((bf16[1024,3,256]{2,0,1:T(8,128)(2,1)}, bf16[256,1024]{1,0:T(8,128)(2,1)}, bf16[1024,1024]{1,0:T(8,128)(2,1)}, bf16[1024,1024]{1,0:T(8,128)(2,1)}, bf16[1024,1536]{1,0:T(8,128)(2,1)}), ...) | async-done | bytes 9437200 | tf_op jit(solution)/shard_map/psum | solution.py:309
  (300 shorter events, 255.5 us)
Async XLA Ops:
  7.2 520.9 %copy-start = (bf16[1024,1024]{1,0:T(8,128)(2,1)S(1)}, bf16[1024,1024]{1,0:T(8,128)(2,1)}, u32[]{:S(2)}) copy-start(bf16[1024,1024]{1,0:T(8,128)(2,1)} %param.25) | copy-start | bytes 6291460
  7.2 97.7 %all-gather.8.cloned.1.call-start = ((), (), s32[]{:S(2)}) async-start(), calls=%async_computation.7 | async-start | bytes 5242880 | tf_op jit(solution)/shard_map/all_gather | solution.py:69
  9.8 9.3 copy-start.33
  12.0 7.7 copy-start.4
  21.3 108.8 %all-gather.10.cloned.1.call-start = ((), (), s32[]{:S(2)}) async-start(), calls=%async_computation.8 | async-start | bytes 3145728 | tf_op jit(solution)/shard_map/all_gather | solution.py:77
  114.4 24.4 %all-gather.18.cloned.1.call-start = ((), (), s32[]{:S(2)}) async-start(), calls=%async_computation.19 | async-start | bytes 3145728 | tf_op jit(solution)/shard_map/all_gather | solution.py:76
  117.2 314.2 %reduce-scatter.8.cloned.1.call-start = ((), (), s32[]{:S(2)}) async-start(), calls=%async_computation.9 | async-start | bytes 5242880 | tf_op jit(solution)/shard_map/reduce_scatter | solution.py:123
  150.0 16.0 copy-start.3
  199.6 16.0 copy-start.3
  249.2 16.0 copy-start.3
  298.8 16.0 copy-start.3
  349.8 81.6 %copy-start.23 = (f32[8,1024]{1,0:T(8,128)S(1)}, f32[8,1024]{1,0:T(8,128)}, u32[]{:S(2)}) copy-start(f32[8,1024]{1,0:T(8,128)} %get-tuple-element.454) | copy-start | bytes 98308
  354.6 80.4 %copy-start.24 = (f32[8,1024]{1,0:T(8,128)S(1)}, f32[8,1024]{1,0:T(8,128)}, u32[]{:S(2)}) copy-start(f32[8,1024]{1,0:T(8,128)} %get-tuple-element.451) | copy-start | bytes 98308
  354.6 80.4 %copy-start.32 = (f32[8,1024]{1,0:T(8,128)S(1)}, f32[8,1024]{1,0:T(8,128)}, u32[]{:S(2)}) copy-start(f32[8,1024]{1,0:T(8,128)} %get-tuple-element.450) | copy-start | bytes 98308
  354.6 163.3 %all-gather.12.cloned.1.call-start = ((), (), s32[]{:S(2)}) async-start(), calls=%async_computation.10 | async-start | bytes 5242880 | tf_op jit(solution)/shard_map/all_gather | solution.py:135
  436.5 174.0 %reduce-scatter.10.cloned.1.call-start = ((), (), s32[]{:S(2)}) async-start(), calls=%async_computation.11 | async-start | bytes 5242880 | tf_op jit(solution)/shard_map/reduce_scatter | solution.py:141
  436.6 259.3 %copy-start.45 = (f32[1024]{0:T(1024)}, f32[1024]{0:T(1024)S(1)}, u32[]{:S(2)}) copy-start(f32[1024]{0:T(1024)S(1)} %convert_element_type.268) | copy-start | bytes 12292
  535.0 75.5 %copy-start.26 = (f32[8,1024]{1,0:T(8,128)S(1)}, f32[8,1024]{1,0:T(8,128)}, u32[]{:S(2)}) copy-start(f32[8,1024]{1,0:T(8,128)} %get-tuple-element.449) | copy-start | bytes 98308
  535.1 160.8 %all-gather.14.cloned.1.call-start = ((), (), s32[]{:S(2)}) async-start(), calls=%async_computation.12 | async-start | bytes 5242880 | tf_op jit(solution)/shard_map/all_gather | solution.py:155
  614.4 178.5 %reduce-scatter.12.cloned.1.call-start = ((), (), s32[]{:S(2)}) async-start(), calls=%async_computation.13 | async-start | bytes 5242880 | tf_op jit(solution)/shard_map/reduce_scatter | solution.py:164
  695.8 15.4 copy-start.54
  717.4 75.5 %copy-start.7 = (f32[1,8,64,1024]{3,2,1,0:T(8,128)S(1)}, f32[1,8,64,1024]{3,2,1,0:T(8,128)}, u32[]{:S(2)}) copy-start(f32[1,8,64,1024]{3,2,1,0:T(8,128)} %copy-done.6) | copy-start | bytes 6291460
  717.4 78.4 %copy-start.17 = (bf16[64,1,8,1024]{3,0,2,1:T(8,128)(2,1)S(1)}, bf16[64,1,8,1024]{3,0,2,1:T(8,128)(2,1)}, u32[]{:S(2)}) copy-start(bf16[64,1,8,1024]{3,0,2,1:T(8,128)(2,1)} %reduce-scatter.8.cloned.1.call-done) | copy-start | bytes 3145732
  717.5 166.9 %all-gather.16.cloned.1.call-start = ((), (), s32[]{:S(2)}) async-start(), calls=%async_computation.14 | async-start | bytes 5242880 | tf_op jit(solution)/shard_map/all_gather | solution.py:179
  800.4 84.0 %copy-start.25 = (bf16[256,1024]{1,0:T(8,128)(2,1)S(1)}, bf16[256,1024]{1,0:T(8,128)(2,1)}, u32[]{:S(2)}) copy-start(bf16[256,1024]{1,0:T(8,128)(2,1)} %param.21) | copy-start | bytes 1572868
  803.0 545.5 %reduce-scatter.14.cloned.1.call-start = ((), (), s32[]{:S(2)}) async-start(), calls=%async_computation.15 | async-start | bytes 3145728 | tf_op jit(solution)/shard_map/reduce_scatter | solution.py:233
  981.9 11.2 copy-start.2
  1090.0 11.2 copy-start.2
  1199.4 11.2 copy-start.2
  1308.8 11.2 copy-start.2
  1336.7 22.3 %reduce-scatter.16.cloned.1.call-start = ((), (), s32[]{:S(2)}) async-start(), calls=%async_computation.16 | async-start | bytes 3145728 | tf_op jit(solution)/shard_map/reduce_scatter | solution.py:239
  1345.6 99.1 %reduce-scatter.18.cloned.1.call-start = ((), (), s32[]{:S(2)}) async-start(), calls=%async_computation.17 | async-start | bytes 5242880 | tf_op jit(solution)/shard_map/reduce_scatter | solution.py:259
  1366.6 9.7 copy-start.46
  1366.6 102.9 %reduce-scatter.20.cloned.1.call-start = ((), (), s32[]{:S(2)}) async-start(), calls=%async_computation.18 | async-start | bytes 122880 | tf_op jit(solution)/shard_map/reduce_scatter | solution.py:284
  1366.8 9.5 copy-start.52
  1376.3 11.1 copy-start.11
  1376.3 11.3 copy-start.16
  1376.3 11.3 copy-start.53
  1387.6 58.6 %copy-start.5 = (f32[1,8,64,1024]{3,2,1,0:T(8,128)S(1)}, f32[1,8,64,1024]{3,2,1,0:T(8,128)}, u32[]{:S(2)}) copy-start(f32[1,8,64,1024]{3,2,1,0:T(8,128)} %param.18) | copy-start | bytes 6291460
  1387.6 58.6 %copy-start.22 = (f32[8,1024]{1,0:T(8,128)S(1)}, f32[8,1024]{1,0:T(8,128)}, u32[]{:S(2)}) copy-start(f32[8,1024]{1,0:T(8,128)} %copy-done.21) | copy-start | bytes 98308
  1387.6 58.6 %copy-start.34 = (f32[8,64]{1,0:T(8,128)S(1)}, f32[8,64]{1,0:T(8,128)}, u32[]{:S(2)}) copy-start(f32[8,64]{1,0:T(8,128)} %copy-done.33) | copy-start | bytes 6148
  1387.6 58.6 %copy-start.37 = (f32[8,64]{1,0:T(8,128)S(1)}, f32[8,64]{1,0:T(8,128)}, u32[]{:S(2)}) copy-start(f32[8,64]{1,0:T(8,128)} %copy-done.36) | copy-start | bytes 6148
  1389.7 59.0 %copy-start.40 = (bf16[8,1024]{1,0:T(8,128)(2,1)S(1)}, bf16[8,1024]{1,0:T(8,128)(2,1)}, u32[]{:S(2)}) copy-start(bf16[8,1024]{1,0:T(8,128)(2,1)} %get-tuple-element.386) | copy-start | bytes 49156
  1389.7 59.0 %copy-start.39 = (bf16[8,1024]{1,0:T(8,128)(2,1)S(1)}, bf16[8,1024]{1,0:T(8,128)(2,1)}, u32[]{:S(2)}) copy-start(bf16[8,1024]{1,0:T(8,128)(2,1)} %get-tuple-element.380) | copy-start | bytes 49156
  1389.7 59.0 %copy-start.38 = (bf16[8,1024]{1,0:T(8,128)(2,1)S(1)}, bf16[8,1024]{1,0:T(8,128)(2,1)}, u32[]{:S(2)}) copy-start(bf16[8,1024]{1,0:T(8,128)(2,1)} %get-tuple-element.384) | copy-start | bytes 49156
  1449.4 20.0 %copy-start.28 = (f32[8,512]{1,0:T(8,128)S(1)}, f32[8,512]{1,0:T(8,128)}, u32[]{:S(2)}) copy-start(f32[8,512]{1,0:T(8,128)} %copy-done.27) | copy-start | bytes 49156
  1449.5 20.0 %copy-start.30 = (f32[8,512]{1,0:T(8,128)S(1)}, f32[8,512]{1,0:T(8,128)}, u32[]{:S(2)}) copy-start(f32[8,512]{1,0:T(8,128)} %copy-done.29) | copy-start | bytes 49156
  1449.5 161.9 %all-reduce.7.cloned.1.call-start = ((), (), s32[]{:S(2)}) async-start(), calls=%async_computation.20 | async-start | bytes 18874368 | tf_op jit(solution)/shard_map/psum | solution.py:309
  (30 other events, 94.2 us)
Sparse Core Ops, SparseCore 0:
  21.4 83.4 all-gather.7
  114.6 9.0 all-gather.9
  125.8 11.7 all-gather.17
  354.7 76.6 reduce-scatter.7
  436.6 81.2 all-gather.11
  535.2 75.2 reduce-scatter.9
  614.6 81.2 all-gather.13
  717.6 75.2 reduce-scatter.11
  803.1 81.2 all-gather.15
  1336.8 8.2 reduce-scatter.13
  1347.9 11.0 reduce-scatter.15
  1366.7 78.0 reduce-scatter.17
  1449.6 19.8 reduce-scatter.19
  1474.8 136.5 all-reduce.6
where the time goes:
time: 1640 us; the launch traced here: 1630 us
  waiting for transfers between devices  739 us (45%)
  matrix products  536 us (33%)
  other arithmetic  244 us (15%)
  local copies, waits for them, and re-layouts  73.1 us (4%)
  blocking collectives  22.1 us (1%)
  between operations  16.4 us (1%)
    dot_general x8, matrix products, masked_scores(): jnp.einsum('bhd,khd->hbk', query_block, keys, preferred_element_type=jnp....  133 us
    convert_element_type x4, other arithmetic, backward_block(): grad_scores = (probability * (grad_prob - inner_sum)).astype(jnp.bfloat16)  110 us
    psum x1, waiting for transfers between devices, body(): lax.psum(grad_w_qkv.astype(jnp.bfloat16), ('dp', 'seq')).astype(jnp.float32)  107 us
    dot_general x4, matrix products, backward_block(): jnp.einsum('bhd,khd->hbk', grad_block, values, preferred_element_type=jnp...  104 us
    all_gather x1, waiting for transfers between devices, body(): attn_all = lax.all_gather(attn_in, 'tensor', axis=2, tiled=True)  83.5 us
    all_gather x1, waiting for transfers between devices, body(): grad_mlp_all = lax.all_gather(grad_mlp_low, 'tensor', axis=2, tiled=True)  81.4 us
    all_gather x1, waiting for transfers between devices, body(): mlp_all = lax.all_gather(mlp_in, 'tensor', axis=2, tiled=True)  81.3 us
    all_gather x1, waiting for transfers between devices, body(): lax.all_gather(grad_branch.astype(jnp.bfloat16), 'tensor', axis=2, tiled=...  81.3 us
  transfers between devices with their start and end apart: 14, of which 11 were waited for; matrix products, arithmetic and copies ran while one was open for 5% of the time, Pallas kernels for 0%

commit v1 on v0

--- a/solution.py
+++ b/solution.py
@@ -306,7 +306,9 @@
         total_w_mod,
         total_b_mod,
     ) = (
-        lax.psum(grad_w_qkv.astype(jnp.bfloat16), ("dp", "seq")).astype(jnp.float32),
+        jnp.sum(lax.all_gather(grad_w_qkv.astype(jnp.bfloat16), ("dp", "seq")), axis=0).astype(
+            jnp.float32
+        ),
         lax.psum(grad_qv_bias.astype(jnp.bfloat16), ("dp", "seq")).astype(jnp.float32),
         lax.psum(grad_w_out.astype(jnp.bfloat16), ("dp", "seq")).astype(jnp.float32),
         lax.psum(out_bias_part.astype(jnp.bfloat16), ("dp", "seq")).astype(jnp.float32),

time: 1640 us -> 1710 us (1.043)
  waiting for transfers between devices: 739 us -> 781 us
    all_gather x0 -> x1, waiting for transfers between devices: none -> 60.9 us  [body(): lax.all_gather(grad_w_qkv.astype(jnp.bfloat16), ('dp', 'seq'))]
    psum x1, waiting for transfers between devices: 107 us -> 82.6 us  [body(): lax.psum(grad_w_out.astype(jnp.bfloat16), ('dp', 'seq')).astype(jnp.float32)]
  transfers between devices with their start and end apart: 14 -> 15, of which waited for: 11 -> 12; matrix products, arithmetic and copies ran while one was open for 5% -> 5% of each run, Pallas kernels for 0% -> 0%
where the time goes in v1:
time: 1710 us; the launch traced here: 1700 us
  waiting for transfers between devices  781 us (46%)
  matrix products  538 us (31%)
  other arithmetic  254 us (15%)
  local copies, waits for them, and re-layouts  83.5 us (5%)
  blocking collectives  22.2 us (1%)
    dot_general x8, matrix products, masked_scores(): jnp.einsum('bhd,khd->hbk', query_block, keys, preferred_element_type=jnp....  133 us
    convert_element_type x4, other arithmetic, backward_block(): grad_scores = (probability * (grad_prob - inner_sum)).astype(jnp.bfloat16)  110 us
    dot_general x4, matrix products, backward_block(): jnp.einsum('bhd,khd->hbk', grad_block, values, preferred_element_type=jnp...  104 us
    all_gather x1, waiting for transfers between devices, body(): attn_all = lax.all_gather(attn_in, 'tensor', axis=2, tiled=True)  83.5 us
    psum x1, waiting for transfers between devices, body(): lax.psum(grad_w_out.astype(jnp.bfloat16), ('dp', 'seq')).astype(jnp.float32)  82.6 us
    all_gather x1, waiting for transfers between devices, body(): grad_mlp_all = lax.all_gather(grad_mlp_low, 'tensor', axis=2, tiled=True)  81.4 us
    all_gather x1, waiting for transfers between devices, body(): lax.all_gather(grad_branch.astype(jnp.bfloat16), 'tensor', axis=2, tiled=...  81.4 us
    all_gather x1, waiting for transfers between devices, body(): mlp_all = lax.all_gather(mlp_in, 'tensor', axis=2, tiled=True)  81.3 us
  transfers between devices with their start and end apart: 15, of which 12 were waited for; matrix products, arithmetic and copies ran while one was open for 5% of the time, Pallas kernels for 0%

profile of v1, /device:TPU:0, one launch (start us, length us, event | category | flops | bytes accessed | tf_op | source)
XLA Modules:
  0.0 1696.8 jit_solution(10161964928065845031)
XLA Ops:
  21.3 83.5 %all-gather.10.cloned.1.call-done = bf16[1,8,256,1024]{3,2,1,0:T(8,128)(2,1)} async-done(((bf16[1,8,64,1024]{3,2,1,0:T(8,128)(2,1)}), bf16[1,8,256,1024]{3,2,1,0:T(8,128)(2,1)}) %all-gather.10.cloned.1.call-update) | async-done | bytes 4194320 | tf_op jit(solution)/shard_map/all_gather | solution.py:69
  147.6 198.2 %while.50 = (s32[]{:T(128)}, bf16[4,512,4,64]{1,3,2,0:T(8,128)(2,1)S(1)}, f32[4,4,512]{2,1,0:T(4,128)S(1)}, s32[4,512]{1,0:T(4,128)S(1)}, s32[]{:T(128)}, /*inde...) while((s32[]{:T(128)}, ...), condition=%wide.region_5.6_spmd.clone.clone, body=%wide.region_2.5_spmd.clone.clone.sunk | while | flops 2252539904 | bytes 122271888 | solution.py:116
  150.1 15.9 fusion.176
  166.0 15.0 fusion.177
  181.1 16.3 fusion.178
  199.6 15.9 fusion.176
  215.5 15.0 fusion.177
  230.5 16.3 fusion.178
  249.0 15.9 fusion.176
  265.0 15.0 fusion.177
  280.0 16.3 fusion.178
  298.5 15.9 fusion.176
  314.4 15.0 fusion.177
  329.5 16.3 fusion.178
  347.6 12.9 reshape.546
  365.4 76.7 %reduce-scatter.8.cloned.1.call-done = bf16[64,1,8,1024]{3,0,2,1:T(8,128)(2,1)} async-done(((bf16[256,1,8,1024]{3,0,2,1:T(8,128)(2,1)}), bf16[64,1,8,1024]{3,0,2,1:T(8,128)(2,1)}) %reduce-scatter.8.cloned.1.call-update) | async-done | bytes 1048592 | tf_op jit(solution)/shard_map/reduce_scatter | solution.py:123
  447.3 81.3 %all-gather.14.cloned.1.call-done = bf16[1,8,256,1024]{3,2,1,0:T(8,128)(2,1)} async-done(((bf16[1,8,64,1024]{3,2,1,0:T(8,128)(2,1)}), bf16[1,8,256,1024]{3,2,1,0:T(8,128)(2,1)}) %all-gather.14.cloned.1.call-update) | async-done | bytes 4194320 | tf_op jit(solution)/shard_map/all_gather | solution.py:135
  546.4 74.8 %reduce-scatter.10.cloned.1.call-done = bf16[64,1,8,1024]{3,0,2,1:T(8,128)(2,1)} async-done(((bf16[256,1,8,1024]{3,0,2,1:T(8,128)(2,1)}), bf16[64,1,8,1024]{3,0,2,1:T(8,128)(2,1)}) %reduce-scatter.10.cloned.1.call-update) | async-done | bytes 1048592 | tf_op jit(solution)/shard_map/reduce_scatter | solution.py:141
  625.2 81.4 %all-gather.16.cloned.1.call-done = bf16[1,8,256,1024]{3,2,1,0:T(8,128)(2,1)} async-done(((bf16[1,8,64,1024]{3,2,1,0:T(8,128)(2,1)}), bf16[1,8,256,1024]{3,2,1,0:T(8,128)(2,1)}) %all-gather.16.cloned.1.call-update) | async-done | bytes 4194320 | tf_op jit(solution)/shard_map/all_gather | solution.py:155
  706.5 13.4 fusion.144
  728.2 75.4 %reduce-scatter.12.cloned.1.call-done = bf16[64,1,8,1024]{3,0,2,1:T(8,128)(2,1)} async-done(((bf16[256,1,8,1024]{3,0,2,1:T(8,128)(2,1)}), bf16[64,1,8,1024]{3,0,2,1:T(8,128)(2,1)}) %reduce-scatter.12.cloned.1.call-update) | async-done | bytes 1048592 | tf_op jit(solution)/shard_map/reduce_scatter | solution.py:164
  813.7 81.4 %all-gather.18.cloned.1.call-done = bf16[1,8,256,1024]{3,2,1,0:T(8,128)(2,1)} async-done(((bf16[1,8,64,1024]{3,2,1,0:T(8,128)(2,1)}), bf16[1,8,256,1024]{3,2,1,0:T(8,128)(2,1)}) %all-gather.18.cloned.1.call-update) | async-done | bytes 4194320 | tf_op jit(solution)/shard_map/all_gather | solution.py:179
  902.8 435.5 %while.51 = (s32[]{:T(128)}, f32[4096,4,64]{0,2,1:T(8,128)}, f32[4096,4,64]{0,2,1:T(8,128)}, bf16[4,512,4,64]{1,3,2,0:T(8,128)(2,1)}, bf16[4,512,4,64]{1,3,2,0:T...) while((s32[]{:T(128)}, f32[4096,4,64]{0,2,1:T(8,128)}, ...), condition=%wide.region_15.16_spmd.clone.clone, body=%wide.region_13.15_spmd.clone.clone.sunk | while | flops 5504305152 | bytes 351639744 | solution.py:221
  905.4 17.3 %fusion.188 = f32[4,512,4096]{2,1,0:T(8,128)} fusion(bf16[4096,4,64]{0,2,1:T(8,128)(2,1)} %get-tuple-element.644, bf16[4,512,4,64]{1,3,2,0:T(8,128)(2,1)} %get-tuple-element.641, s32[]{:T(128)S(6)} %copy.131), kind=kOutput, calls=%fused_computation.48.clone.1 | convolution fusion | flops 1073741824 | bytes 35913732 | tf_op jit(solution)/shard_map/while/body/eval_jaxpr/while/body/eval_jaxpr/bhd,khd->hbk/dot_general | solution.py:93
  922.7 16.5 fusion.190
  939.2 25.9 %multiply_reduce_fusion.6 = (f32[4,512]{1,0:T(4,128)S(1)}, f32[4,512,4096]{2,1,0:T(8,128)}) fusion(f32[4,512,4096]{2,1,0:T(8,128)} %fusion.188, f32[4,512]{1,0:T(4,128)S(1)} %dynamic-slice_bitcast_fusion.2, pred[512,4096]{1,0:T(8,128)(4,1)S(1)} %compare_or_fusion.5, bf16[4096,4,64]{0,2,1:T(8,128)(2,1)} %get-tuple-element.647, ...), kind=kOutput, calls=%fused_computation.29.clone.1 | convolution fusion | flops 1115682816 | bytes 71581696 | tf_op jit(solution)/shard_map/while/body/eval_jaxpr/while/body/eval_jaxpr/bhd,khd->hbk/dot_general | solution.py:196
  965.1 27.6 %multiply_convert_fusion.10 = bf16[4,512,4096]{2,1,0:T(8,128)(2,1)} fusion(f32[4,512,4096]{2,1,0:T(8,128)} %get-tuple-element.582, f32[4,512,4096]{2,1,0:T(8,128)} %fusion.188, f32[4,512]{1,0:T(4,128)S(1)} %get-tuple-element.583, f32[4,512]{1,0:T(4,128)S(1)} %dynamic-slice_bitcast_fusion.2, pred[512,4096]{1,0:T(8,128)(4,1)S(1)} %compare_or_fusion.5), kind=kLoop, calls=%fused_computation.28.clone.1 | loop fusion | flops 50331648 | bytes 85999616 | tf_op jit(solution)/shard_map/while/body/eval_jaxpr/while/body/eval_jaxpr/convert_element_type | solution.py:200
  1012.3 17.3 %fusion.188 = f32[4,512,4096]{2,1,0:T(8,128)} fusion(bf16[4096,4,64]{0,2,1:T(8,128)(2,1)} %get-tuple-element.644, bf16[4,512,4,64]{1,3,2,0:T(8,128)(2,1)} %get-tuple-element.641, s32[]{:T(128)S(6)} %copy.131), kind=kOutput, calls=%fused_computation.48.clone.1 | convolution fusion | flops 1073741824 | bytes 35913732 | tf_op jit(solution)/shard_map/while/body/eval_jaxpr/while/body/eval_jaxpr/bhd,khd->hbk/dot_general | solution.py:93
  1029.6 17.7 %fusion.190 = f32[4096,4,64]{0,2,1:T(8,128)} fusion(f32[4,512,4096]{2,1,0:T(8,128)} %fusion.188, f32[4,512]{1,0:T(4,128)S(1)} %dynamic-slice_bitcast_fusion.2, pred[512,4096]{1,0:T(8,128)(4,1)S(1)} %compare_or_fusion.5, f32[4096,4,64]{0,2,1:T(8,128)} %get-tuple-element.626, pred[]{:T(512)S(6)} %compare.9, ...), kind=kOutput, calls=%fused_computation.39.clone.1 | convolution fusion | flops 1109393408 | bytes 44310532 | tf_op jit(solution)/shard_map/while/body/eval_jaxpr/while/body/eval_jaxpr/hbk,bhd->khd/dot_general | solution.py:212
  1047.3 25.9 %multiply_reduce_fusion.6 = (f32[4,512]{1,0:T(4,128)S(1)}, f32[4,512,4096]{2,1,0:T(8,128)}) fusion(f32[4,512,4096]{2,1,0:T(8,128)} %fusion.188, f32[4,512]{1,0:T(4,128)S(1)} %dynamic-slice_bitcast_fusion.2, pred[512,4096]{1,0:T(8,128)(4,1)S(1)} %compare_or_fusion.5, bf16[4096,4,64]{0,2,1:T(8,128)(2,1)} %get-tuple-element.647, ...), kind=kOutput, calls=%fused_computation.29.clone.1 | convolution fusion | flops 1115682816 | bytes 71581696 | tf_op jit(solution)/shard_map/while/body/eval_jaxpr/while/body/eval_jaxpr/bhd,khd->hbk/dot_general | solution.py:196
  1073.2 27.6 %multiply_convert_fusion.10 = bf16[4,512,4096]{2,1,0:T(8,128)(2,1)} fusion(f32[4,512,4096]{2,1,0:T(8,128)} %get-tuple-element.582, f32[4,512,4096]{2,1,0:T(8,128)} %fusion.188, f32[4,512]{1,0:T(4,128)S(1)} %get-tuple-element.583, f32[4,512]{1,0:T(4,128)S(1)} %dynamic-slice_bitcast_fusion.2, pred[512,4096]{1,0:T(8,128)(4,1)S(1)} %compare_or_fusion.5), kind=kLoop, calls=%fused_computation.28.clone.1 | loop fusion | flops 50331648 | bytes 85999616 | tf_op jit(solution)/shard_map/while/body/eval_jaxpr/while/body/eval_jaxpr/convert_element_type | solution.py:200
  1100.8 10.2 fusion.191
  1121.7 17.3 %fusion.188 = f32[4,512,4096]{2,1,0:T(8,128)} fusion(bf16[4096,4,64]{0,2,1:T(8,128)(2,1)} %get-tuple-element.644, bf16[4,512,4,64]{1,3,2,0:T(8,128)(2,1)} %get-tuple-element.641, s32[]{:T(128)S(6)} %copy.131), kind=kOutput, calls=%fused_computation.48.clone.1 | convolution fusion | flops 1073741824 | bytes 35913732 | tf_op jit(solution)/shard_map/while/body/eval_jaxpr/while/body/eval_jaxpr/bhd,khd->hbk/dot_general | solution.py:93
  1139.0 17.7 %fusion.190 = f32[4096,4,64]{0,2,1:T(8,128)} fusion(f32[4,512,4096]{2,1,0:T(8,128)} %fusion.188, f32[4,512]{1,0:T(4,128)S(1)} %dynamic-slice_bitcast_fusion.2, pred[512,4096]{1,0:T(8,128)(4,1)S(1)} %compare_or_fusion.5, f32[4096,4,64]{0,2,1:T(8,128)} %get-tuple-element.626, pred[]{:T(512)S(6)} %compare.9, ...), kind=kOutput, calls=%fused_computation.39.clone.1 | convolution fusion | flops 1109393408 | bytes 44310532 | tf_op jit(solution)/shard_map/while/body/eval_jaxpr/while/body/eval_jaxpr/hbk,bhd->khd/dot_general | solution.py:212
  1156.7 25.9 %multiply_reduce_fusion.6 = (f32[4,512]{1,0:T(4,128)S(1)}, f32[4,512,4096]{2,1,0:T(8,128)}) fusion(f32[4,512,4096]{2,1,0:T(8,128)} %fusion.188, f32[4,512]{1,0:T(4,128)S(1)} %dynamic-slice_bitcast_fusion.2, pred[512,4096]{1,0:T(8,128)(4,1)S(1)} %compare_or_fusion.5, bf16[4096,4,64]{0,2,1:T(8,128)(2,1)} %get-tuple-element.647, ...), kind=kOutput, calls=%fused_computation.29.clone.1 | convolution fusion | flops 1115682816 | bytes 71581696 | tf_op jit(solution)/shard_map/while/body/eval_jaxpr/while/body/eval_jaxpr/bhd,khd->hbk/dot_general | solution.py:196
  1182.6 27.6 %multiply_convert_fusion.10 = bf16[4,512,4096]{2,1,0:T(8,128)(2,1)} fusion(f32[4,512,4096]{2,1,0:T(8,128)} %get-tuple-element.582, f32[4,512,4096]{2,1,0:T(8,128)} %fusion.188, f32[4,512]{1,0:T(4,128)S(1)} %get-tuple-element.583, f32[4,512]{1,0:T(4,128)S(1)} %dynamic-slice_bitcast_fusion.2, pred[512,4096]{1,0:T(8,128)(4,1)S(1)} %compare_or_fusion.5), kind=kLoop, calls=%fused_computation.28.clone.1 | loop fusion | flops 50331648 | bytes 85999616 | tf_op jit(solution)/shard_map/while/body/eval_jaxpr/while/body/eval_jaxpr/convert_element_type | solution.py:200
  1210.2 10.1 fusion.191
  1231.0 17.3 %fusion.188 = f32[4,512,4096]{2,1,0:T(8,128)} fusion(bf16[4096,4,64]{0,2,1:T(8,128)(2,1)} %get-tuple-element.644, bf16[4,512,4,64]{1,3,2,0:T(8,128)(2,1)} %get-tuple-element.641, s32[]{:T(128)S(6)} %copy.131), kind=kOutput, calls=%fused_computation.48.clone.1 | convolution fusion | flops 1073741824 | bytes 35913732 | tf_op jit(solution)/shard_map/while/body/eval_jaxpr/while/body/eval_jaxpr/bhd,khd->hbk/dot_general | solution.py:93
  1248.3 17.7 %fusion.190 = f32[4096,4,64]{0,2,1:T(8,128)} fusion(f32[4,512,4096]{2,1,0:T(8,128)} %fusion.188, f32[4,512]{1,0:T(4,128)S(1)} %dynamic-slice_bitcast_fusion.2, pred[512,4096]{1,0:T(8,128)(4,1)S(1)} %compare_or_fusion.5, f32[4096,4,64]{0,2,1:T(8,128)} %get-tuple-element.626, pred[]{:T(512)S(6)} %compare.9, ...), kind=kOutput, calls=%fused_computation.39.clone.1 | convolution fusion | flops 1109393408 | bytes 44310532 | tf_op jit(solution)/shard_map/while/body/eval_jaxpr/while/body/eval_jaxpr/hbk,bhd->khd/dot_general | solution.py:212
  1266.0 25.9 %multiply_reduce_fusion.6 = (f32[4,512]{1,0:T(4,128)S(1)}, f32[4,512,4096]{2,1,0:T(8,128)}) fusion(f32[4,512,4096]{2,1,0:T(8,128)} %fusion.188, f32[4,512]{1,0:T(4,128)S(1)} %dynamic-slice_bitcast_fusion.2, pred[512,4096]{1,0:T(8,128)(4,1)S(1)} %compare_or_fusion.5, bf16[4096,4,64]{0,2,1:T(8,128)(2,1)} %get-tuple-element.647, ...), kind=kOutput, calls=%fused_computation.29.clone.1 | convolution fusion | flops 1115682816 | bytes 71581696 | tf_op jit(solution)/shard_map/while/body/eval_jaxpr/while/body/eval_jaxpr/bhd,khd->hbk/dot_general | solution.py:196
  1292.0 27.6 %multiply_convert_fusion.10 = bf16[4,512,4096]{2,1,0:T(8,128)(2,1)} fusion(f32[4,512,4096]{2,1,0:T(8,128)} %get-tuple-element.582, f32[4,512,4096]{2,1,0:T(8,128)} %fusion.188, f32[4,512]{1,0:T(4,128)S(1)} %get-tuple-element.583, f32[4,512]{1,0:T(4,128)S(1)} %dynamic-slice_bitcast_fusion.2, pred[512,4096]{1,0:T(8,128)(4,1)S(1)} %compare_or_fusion.5), kind=kLoop, calls=%fused_computation.28.clone.1 | loop fusion | flops 50331648 | bytes 85999616 | tf_op jit(solution)/shard_map/while/body/eval_jaxpr/while/body/eval_jaxpr/convert_element_type | solution.py:200
  1359.0 10.5 reduce-scatter.16.cloned.1.call-done
  1386.6 11.0 bitcast_convert_fusion.1
  1397.9 57.3 %reduce-scatter.18.cloned.1.call-done = bf16[64,1,8,1024]{3,0,2,1:T(8,128)(2,1)} async-done(((bf16[256,1,8,1024]{3,0,2,1:T(8,128)(2,1)}), bf16[64,1,8,1024]{3,0,2,1:T(8,128)(2,1)}) %reduce-scatter.18.cloned.1.call-update) | async-done | bytes 1048592 | tf_op jit(solution)/shard_map/reduce_scatter | solution.py:259
  1464.6 15.2 reduce-scatter.20.cloned.1.call-done
  1505.8 13.2 all-reduce.2
  1522.0 82.6 %all-reduce.7.cloned.1.call-done = (bf16[256,1024]{1,0:T(8,128)(2,1)}, bf16[1024,1024]{1,0:T(8,128)(2,1)}, bf16[1024,1024]{1,0:T(8,128)(2,1)}, bf16[1024,1536]{1,0:T(8,128)(2,1)}) async-done(((bf16[256,1024]{1,0:T(8,128)(2,1)}, bf16[1024,1024]{1,0:T(8,128)(2,1)}, bf16[1024,1024]{1,0:T(8,128)(2,1)}, bf16[1024,1536]{1,0:T(8,128)(2,1)}), (bf16[256,1024]{1,0:T(8,128)(2,1)}, bf16[1024,1024]{1,0:T(8,128)(2,1)}, ...) | async-done | bytes 7864336 | tf_op jit(solution)/shard_map/psum | solution.py:313
  1617.7 60.9 %all-gather.22.cloned.1.call-done = bf16[8192,3,256]{2,0,1:T(8,128)(2,1)} async-done(((bf16[1024,3,256]{2,0,1:T(8,128)(2,1)}), bf16[8192,3,256]{2,0,1:T(8,128)(2,1)}) %all-gather.22.cloned.1.call-update) | async-done | bytes 12582928 | tf_op jit(solution)/shard_map/all_gather | solution.py:309
  (298 shorter events, 285.6 us)
Async XLA Ops:
  7.2 531.6 %copy-start = (bf16[1024,1024]{1,0:T(8,128)(2,1)S(1)}, bf16[1024,1024]{1,0:T(8,128)(2,1)}, u32[]{:S(2)}) copy-start(bf16[1024,1024]{1,0:T(8,128)(2,1)} %param.25) | copy-start | bytes 6291460
  7.2 97.7 %all-gather.10.cloned.1.call-start = ((), (), s32[]{:S(2)}) async-start(), calls=%async_computation.7 | async-start | bytes 5242880 | tf_op jit(solution)/shard_map/all_gather | solution.py:69
  9.8 9.3 copy-start.31
  21.2 108.8 %all-gather.12.cloned.1.call-start = ((), (), s32[]{:S(2)}) async-start(), calls=%async_computation.8 | async-start | bytes 3145728 | tf_op jit(solution)/shard_map/all_gather | solution.py:77
  114.4 24.4 %all-gather.20.cloned.1.call-start = ((), (), s32[]{:S(2)}) async-start(), calls=%async_computation.19 | async-start | bytes 3145728 | tf_op jit(solution)/shard_map/all_gather | solution.py:76
  117.2 324.9 %reduce-scatter.8.cloned.1.call-start = ((), (), s32[]{:S(2)}) async-start(), calls=%async_computation.9 | async-start | bytes 5242880 | tf_op jit(solution)/shard_map/reduce_scatter | solution.py:123
  150.1 15.9 copy-start.3
  199.6 15.9 copy-start.3
  249.0 15.9 copy-start.3
  298.5 15.9 copy-start.3
  360.5 81.6 %copy-start.21 = (f32[8,1024]{1,0:T(8,128)S(1)}, f32[8,1024]{1,0:T(8,128)}, u32[]{:S(2)}) copy-start(f32[8,1024]{1,0:T(8,128)} %get-tuple-element.453) | copy-start | bytes 98308
  365.3 80.4 %copy-start.22 = (f32[8,1024]{1,0:T(8,128)S(1)}, f32[8,1024]{1,0:T(8,128)}, u32[]{:S(2)}) copy-start(f32[8,1024]{1,0:T(8,128)} %get-tuple-element.450) | copy-start | bytes 98308
  365.3 80.4 %copy-start.30 = (f32[8,1024]{1,0:T(8,128)S(1)}, f32[8,1024]{1,0:T(8,128)}, u32[]{:S(2)}) copy-start(f32[8,1024]{1,0:T(8,128)} %get-tuple-element.449) | copy-start | bytes 98308
  365.3 163.3 %all-gather.14.cloned.1.call-start = ((), (), s32[]{:S(2)}) async-start(), calls=%async_computation.10 | async-start | bytes 5242880 | tf_op jit(solution)/shard_map/all_gather | solution.py:135
  447.2 174.0 %reduce-scatter.10.cloned.1.call-start = ((), (), s32[]{:S(2)}) async-start(), calls=%async_computation.11 | async-start | bytes 5242880 | tf_op jit(solution)/shard_map/reduce_scatter | solution.py:141
  447.3 259.3 %copy-start.43 = (f32[1024]{0:T(1024)}, f32[1024]{0:T(1024)S(1)}, u32[]{:S(2)}) copy-start(f32[1024]{0:T(1024)S(1)} %convert_element_type.270) | copy-start | bytes 12292
  545.7 75.5 %copy-start.24 = (f32[8,1024]{1,0:T(8,128)S(1)}, f32[8,1024]{1,0:T(8,128)}, u32[]{:S(2)}) copy-start(f32[8,1024]{1,0:T(8,128)} %get-tuple-element.448) | copy-start | bytes 98308
  545.7 160.8 %all-gather.16.cloned.1.call-start = ((), (), s32[]{:S(2)}) async-start(), calls=%async_computation.12 | async-start | bytes 5242880 | tf_op jit(solution)/shard_map/all_gather | solution.py:155
  625.1 178.4 %reduce-scatter.12.cloned.1.call-start = ((), (), s32[]{:S(2)}) async-start(), calls=%async_computation.13 | async-start | bytes 5242880 | tf_op jit(solution)/shard_map/reduce_scatter | solution.py:164
  706.5 15.4 copy-start.51
  728.1 75.4 %copy-start.7 = (f32[1,8,64,1024]{3,2,1,0:T(8,128)S(1)}, f32[1,8,64,1024]{3,2,1,0:T(8,128)}, u32[]{:S(2)}) copy-start(f32[1,8,64,1024]{3,2,1,0:T(8,128)} %copy-done.6) | copy-start | bytes 6291460
  728.1 78.4 %copy-start.16 = (bf16[64,1,8,1024]{3,0,2,1:T(8,128)(2,1)S(1)}, bf16[64,1,8,1024]{3,0,2,1:T(8,128)(2,1)}, u32[]{:S(2)}) copy-start(bf16[64,1,8,1024]{3,0,2,1:T(8,128)(2,1)} %reduce-scatter.8.cloned.1.call-done) | copy-start | bytes 3145732
  728.1 166.9 %all-gather.18.cloned.1.call-start = ((), (), s32[]{:S(2)}) async-start(), calls=%async_computation.14 | async-start | bytes 5242880 | tf_op jit(solution)/shard_map/all_gather | solution.py:179
  811.0 84.0 %copy-start.23 = (bf16[256,1024]{1,0:T(8,128)(2,1)S(1)}, bf16[256,1024]{1,0:T(8,128)(2,1)}, u32[]{:S(2)}) copy-start(bf16[256,1024]{1,0:T(8,128)(2,1)} %param.21) | copy-start | bytes 1572868
  813.6 545.4 %reduce-scatter.14.cloned.1.call-start = ((), (), s32[]{:S(2)}) async-start(), calls=%async_computation.15 | async-start | bytes 3145728 | tf_op jit(solution)/shard_map/reduce_scatter | solution.py:233
  992.7 11.2 copy-start.2
  1100.8 11.2 copy-start.2
  1210.2 11.2 copy-start.2
  1319.6 11.2 copy-start.2
  1347.2 22.3 %reduce-scatter.16.cloned.1.call-start = ((), (), s32[]{:S(2)}) async-start(), calls=%async_computation.16 | async-start | bytes 3145728 | tf_op jit(solution)/shard_map/reduce_scatter | solution.py:239
  1356.1 99.1 %reduce-scatter.18.cloned.1.call-start = ((), (), s32[]{:S(2)}) async-start(), calls=%async_computation.17 | async-start | bytes 5242880 | tf_op jit(solution)/shard_map/reduce_scatter | solution.py:259
  1377.0 9.6 copy-start.44
  1377.0 102.7 %reduce-scatter.20.cloned.1.call-start = ((), (), s32[]{:S(2)}) async-start(), calls=%async_computation.18 | async-start | bytes 122880 | tf_op jit(solution)/shard_map/reduce_scatter | solution.py:284
  1377.1 9.5 copy-start.50
  1386.6 11.1 copy-start.11
  1386.6 70.1 %copy-start.5 = (f32[1,8,64,1024]{3,2,1,0:T(8,128)S(1)}, f32[1,8,64,1024]{3,2,1,0:T(8,128)}, u32[]{:S(2)}) copy-start(f32[1,8,64,1024]{3,2,1,0:T(8,128)} %param.18) | copy-start | bytes 6291460
  1386.6 70.1 %copy-start.20 = (f32[8,1024]{1,0:T(8,128)S(1)}, f32[8,1024]{1,0:T(8,128)}, u32[]{:S(2)}) copy-start(f32[8,1024]{1,0:T(8,128)} %copy-done.19) | copy-start | bytes 98308
  1386.6 70.1 %copy-start.32 = (f32[8,64]{1,0:T(8,128)S(1)}, f32[8,64]{1,0:T(8,128)}, u32[]{:S(2)}) copy-start(f32[8,64]{1,0:T(8,128)} %copy-done.31) | copy-start | bytes 6148
  1386.6 70.1 %copy-start.35 = (f32[8,64]{1,0:T(8,128)S(1)}, f32[8,64]{1,0:T(8,128)}, u32[]{:S(2)}) copy-start(f32[8,64]{1,0:T(8,128)} %copy-done.34) | copy-start | bytes 6148
  1397.7 61.3 %copy-start.38 = (bf16[8,1024]{1,0:T(8,128)(2,1)S(1)}, bf16[8,1024]{1,0:T(8,128)(2,1)}, u32[]{:S(2)}) copy-start(bf16[8,1024]{1,0:T(8,128)(2,1)} %get-tuple-element.386) | copy-start | bytes 49156
  1397.7 61.3 %copy-start.37 = (bf16[8,1024]{1,0:T(8,128)(2,1)S(1)}, bf16[8,1024]{1,0:T(8,128)(2,1)}, u32[]{:S(2)}) copy-start(bf16[8,1024]{1,0:T(8,128)(2,1)} %get-tuple-element.380) | copy-start | bytes 49156
  1397.7 61.4 %copy-start.36 = (bf16[8,1024]{1,0:T(8,128)(2,1)S(1)}, bf16[8,1024]{1,0:T(8,128)(2,1)}, u32[]{:S(2)}) copy-start(bf16[8,1024]{1,0:T(8,128)(2,1)} %get-tuple-element.384) | copy-start | bytes 49156
  1459.7 20.0 %copy-start.26 = (f32[8,512]{1,0:T(8,128)S(1)}, f32[8,512]{1,0:T(8,128)}, u32[]{:S(2)}) copy-start(f32[8,512]{1,0:T(8,128)} %copy-done.25) | copy-start | bytes 49156
  1459.7 20.0 %copy-start.28 = (f32[8,512]{1,0:T(8,128)S(1)}, f32[8,512]{1,0:T(8,128)}, u32[]{:S(2)}) copy-start(f32[8,512]{1,0:T(8,128)} %copy-done.27) | copy-start | bytes 49156
  1459.7 144.9 %all-reduce.7.cloned.1.call-start = ((), (), s32[]{:S(2)}) async-start(), calls=%async_computation.21 | async-start | bytes 15728640 | tf_op jit(solution)/shard_map/psum | solution.py:313
  1483.2 8.8 copy-start.40
  1483.2 195.3 %all-gather.22.cloned.1.call-start = ((), (), s32[]{:S(2)}) async-start(), calls=%async_computation.20 | async-start | bytes 14155776 | tf_op jit(solution)/shard_map/all_gather | solution.py:309
  1678.5 11.4 copy-start.1
  (28 other events, 108.2 us)
Sparse Core Ops, SparseCore 0:
  21.4 83.4 all-gather.9
  114.6 9.0 all-gather.11
  125.8 11.7 all-gather.19
  365.4 76.6 reduce-scatter.7
  447.3 81.2 all-gather.13
  545.9 75.2 reduce-scatter.9
  625.2 81.2 all-gather.15
  728.3 75.2 reduce-scatter.11
  813.7 81.2 all-gather.17
  1347.3 8.2 reduce-scatter.13
  1358.4 11.0 reduce-scatter.15
  1377.1 78.0 reduce-scatter.17
  1459.8 19.8 reduce-scatter.19
  1484.5 120.1 all-reduce.6
  1606.4 72.1 all-gather.21
